TPU v7x, 256 devices: a whole 4x4x8 slice. The times are simulated.
256 devices in a mesh: row: 8 (over z_hi, core), col: 32 (over y, z_lo, x).
Axes of the slice: x: 4, y: 4, z: 8 (z_hi: 4, z_lo: 2; z = z_hi * 2 + z_lo), core: 2. Of those that a mesh axis runs over, the one named last changes fastest.
Arguments:
- features: bfloat16 [65536, 512], P('col'), may hold values from -6 to 6
- weight_raw: bfloat16 [512, 512], P('col'), may hold values from -0.0234375 to 0.0234375
- direction_raw: bfloat16 [512, 512], P('col'), may hold values from -0.0014648438 to 0.0014648438
- panel_index: int32 [4096], P('row'), may hold values from 0 to 65535, as said below
- labels: int32 [4096, 65536], P('row', 'col'), may hold values 0 or 1
Outputs:
- gradient: float32 [512, 512], P('col')
- hess_vec: float32 [512, 512], P('col')
Inputs may be any that keep to these rules, and one draw needn't show every extreme that they name: `panel_index`: distinct compounds; the largest entry is 65535.
All inputs are finite; a program needn't handle non-finite values. No bound on the sum of `labels` on one device may be relied on, other than what follows from the above.
Results may differ from a plain program's by a relative error of at most 0.0033.
Values may be sent and summed in bfloat16 or wider, within the bound.
No kernel may reach another device: no remote copies, remote signals or barrier semaphores. Data moves between devices by JAX's collectives and lax.ppermute only.
A program may use at most 64 MiB of HBM per device.

v0:
```python
import math

import jax
import jax.numpy as jnp
from jax import lax
from jax.sharding import PartitionSpec as P


def symmetric(matrix):
    as_float = matrix.astype(jnp.float32)
    return ((as_float + as_float.T) * 0.5).astype(jnp.bfloat16)


def shards(features, weight_raw, direction_raw, panel_index, labels):
    weight_full, direction_full = (
        lax.all_gather(weight_raw, "col", axis=0, tiled=True),
        lax.all_gather(direction_raw, "col", axis=0, tiled=True),
    )
    weight_sym = symmetric(weight_full)
    direction_sym = symmetric(direction_full)
    col_count = features.shape[0]
    offset = lax.axis_index("col") * col_count
    local_pos = panel_index - offset
    is_owned = (local_pos >= 0) & (local_pos < col_count)
    picked = jnp.take(features, jnp.clip(local_pos, 0, col_count - 1), axis=0)
    picked = jnp.where(is_owned[:, None], picked.astype(jnp.float32), 0.0)
    panel_rows = lax.psum(picked.astype(jnp.bfloat16), "col")
    panel_count = panel_rows.shape[0]
    proj_weight = jnp.dot(panel_rows, weight_sym, preferred_element_type=jnp.float32)
    proj_direction = jnp.dot(panel_rows, direction_sym, preferred_element_type=jnp.float32)
    projected = jnp.concatenate([proj_weight, proj_direction], axis=0).astype(jnp.bfloat16)
    pair_vals = lax.dot_general(
        projected, features, (((1,), (1,)), ((), ())), preferred_element_type=jnp.float32
    )
    margin = pair_vals[:panel_count]
    change = pair_vals[panel_count:]
    probability = jax.nn.sigmoid(margin)
    residual_weight = probability - labels.astype(jnp.float32)
    curvature_weight = probability * (1.0 - probability) * change
    pair_weights = jnp.concatenate([residual_weight, curvature_weight], axis=0).astype(jnp.bfloat16)
    col_sums = jnp.dot(pair_weights, features, preferred_element_type=jnp.float32)
    resid_sums = col_sums[:panel_count]
    curv_sums = col_sums[panel_count:]
    panel_float = panel_rows.astype(jnp.float32)
    pair_scale = 1.0 / math.sqrt(
        panel_count * lax.axis_size("row") * col_count * lax.axis_size("col")
    )
    highest = lax.Precision.HIGHEST
    grad_half = jnp.dot(
        panel_float.T, resid_sums, preferred_element_type=jnp.float32, precision=highest
    )
    curv_half = jnp.dot(
        panel_float.T, curv_sums, preferred_element_type=jnp.float32, precision=highest
    )
    grad_term = (grad_half + grad_half.T) * (0.5 * pair_scale)
    curv_term = (curv_half + curv_half.T) * (0.5 * pair_scale)
    summed = lax.psum((grad_term, curv_term), "row")
    gradient, hess_vec = (
        lax.psum_scatter(summed[0], "col", scatter_dimension=0, tiled=True),
        lax.psum_scatter(summed[1], "col", scatter_dimension=0, tiled=True),
    )
    return (gradient, hess_vec)


def solution(mesh):
    return jax.shard_map(
        shards,
        mesh=mesh,
        in_specs=(P("col", None), P("col", None), P("col", None), P("row"), P("row", "col")),
        out_specs=(P("col", None), P("col", None)),
        check_vma=False,
    )
```

profile of v0, /device:TPU:1, one launch (start us, length us, event | category | flops | bytes accessed | tf_op | source)
XLA Modules:
  0.0 745.6 jit_solution(11462926430872568928)
XLA Ops:
  7.2 0.0 all-reduce.4.cloned.1.call-start
  7.2 0.8 compare_and_fusion
  8.1 0.7 copy-done
  8.8 2.0 gather_fusion
  10.8 1.0 select_convert_fusion
  11.8 0.0 reduce-scatter.3.cloned.1.call-start
  11.8 72.3 %all_gather.7 = bf16[512,512]{1,0:T(8,128)(2,1)S(1)} all-gather(bf16[16,512]{1,0:T(8,128)(2,1)S(1)} %copy-done.5), channel_id=1, replica_groups=mesh['row'=8,'col'=32] {'col'}, dimensions={0}, use_global_device_ids=true | all-gather | bytes 540672 | tf_op jit(solution)/shard_map/all_gather | solution.py:17
  84.2 0.2 copy.18
  84.4 1.2 copy.19
  85.6 65.7 %all_gather.6 = bf16[512,512]{1,0:T(8,128)(2,1)S(1)} all-gather(bf16[16,512]{1,0:T(8,128)(2,1)S(1)} %copy-done.6), channel_id=1, replica_groups=mesh['row'=8,'col'=32] {'col'}, dimensions={0}, use_global_device_ids=true | all-gather | bytes 540672 | tf_op jit(solution)/shard_map/all_gather | solution.py:16
  151.2 1.2 copy.17
  152.5 153.6 %all-reduce.4.cloned.1.call-done = bf16[512,512]{1,0:T(8,128)(2,1)} async-done(((bf16[512,512]{1,0:T(8,128)(2,1)}), bf16[512,512]{1,0:T(8,128)(2,1)}) %all-reduce.4.cloned.1.call-update) | async-done | bytes 524304 | tf_op jit(solution)/shard_map/psum | solution.py:27
  306.1 2.0 convolution_convert_fusion
  308.1 0.5 convolution_convert_fusion.1
  308.6 2.4 fusion.13
  311.0 1.7 subtract_convert_fusion
  312.7 2.3 fusion.5
  315.0 1.3 copy-done.4
  316.4 1.1 fusion.11
  317.5 1.3 copy.20
  318.8 2.4 fusion.18
  321.2 0.0 reduce-scatter.5.cloned.1.call-start
  321.3 2.5 fusion.9
  323.8 1.3 copy.21
  325.1 2.4 fusion.17
  327.5 0.0 all-reduce.6.cloned.1.call-start
  327.6 152.4 %reduce-scatter.3.cloned.1.call-done = f32[16,512]{1,0:T(8,128)} async-done(((f32[512,512]{1,0:T(8,128)}), f32[16,512]{1,0:T(8,128)}) %reduce-scatter.3.cloned.1.call-update) | async-done | bytes 32784 | tf_op jit(solution)/shard_map/reduce_scatter | solution.py:59
  479.9 161.8 %reduce-scatter.5.cloned.1.call-done = f32[16,512]{1,0:T(8,128)} async-done(((f32[512,512]{1,0:T(8,128)}), f32[16,512]{1,0:T(8,128)}) %reduce-scatter.5.cloned.1.call-update) | async-done | bytes 32784 | tf_op jit(solution)/shard_map/reduce_scatter | solution.py:60
  641.7 0.0 all-reduce.6.cloned.1.call-update
  641.7 94.6 %all-reduce.6.cloned.1.call-done = (f32[16,512]{1,0:T(8,128)}, f32[16,512]{1,0:T(8,128)}) async-done(((f32[16,512]{1,0:T(8,128)}, f32[16,512]{1,0:T(8,128)}), (f32[16,512]{1,0:T(8,128)}, f32[16,512]{1,0:T(8,128)})) %all-reduce.6.cloned.1.call-update) | async-done | bytes 65552 | tf_op jit(solution)/shard_map/psum | solution.py:57
  736.3 1.4 copy.25
  737.7 1.4 copy.26
  (16 shorter events, 0.1 us)
Async XLA Ops:
  7.2 1.6 copy-start
  7.2 298.9 %all-reduce.4.cloned.1.call-start = ((), (), s32[]{:S(2)}) async-start(), calls=%async_computation.2 | async-start | bytes 1048576 | tf_op jit(solution)/shard_map/psum | solution.py:27
  8.8 3.1 copy-start.5
  11.8 73.8 %copy-start.6 = (bf16[16,512]{1,0:T(8,128)(2,1)S(1)}, bf16[16,512]{1,0:T(8,128)(2,1)}, u32[]{:S(2)}) copy-start(bf16[16,512]{1,0:T(8,128)(2,1)} %param.6) | copy-start | bytes 49156
  11.8 468.2 %reduce-scatter.3.cloned.1.call-start = ((), (), s32[]{:S(2)}) async-start(), calls=%async_computation.3 | async-start | bytes 1081344 | tf_op jit(solution)/shard_map/reduce_scatter | solution.py:59
  306.1 2.0 copy-start.1
  306.1 2.0 copy-start.2
  308.6 2.4 copy-start.3
  315.0 1.3 copy-start.4
  321.2 320.4 %reduce-scatter.5.cloned.1.call-start = ((), (), s32[]{:S(2)}) async-start(), calls=%async_computation.4 | async-start | bytes 1081344 | tf_op jit(solution)/shard_map/reduce_scatter | solution.py:60
  327.5 408.8 %all-reduce.6.cloned.1.call-start = ((), (), s32[]{:S(2)}) async-start(), calls=%async_computation.5 | async-start | bytes 131072 | tf_op jit(solution)/shard_map/psum | solution.py:57
Sparse Core Ops, SparseCore 0:
  11.9 294.1 all-reduce.3
  321.4 158.5 reduce-scatter.2
  482.4 159.2 reduce-scatter.4
  644.4 91.8 all-reduce.5
where the time goes:
time: 746 us
  waiting for transfers between devices  562 us (75%)
  blocking collectives  138 us (18%)
  between operations  13.9 us (2%)
  local copies, waits for them, and re-layouts  12 us (2%)
  matrix products  10.7 us (1%)
  other arithmetic  8.43 us (1%)
    reduce_scatter x1, waiting for transfers between devices, shards(): lax.psum_scatter(summed[1], 'col', scatter_dimension=0, tiled=True)  162 us
    psum x1, waiting for transfers between devices, shards(): panel_rows = lax.psum(picked.astype(jnp.bfloat16), 'col')  154 us
    reduce_scatter x1, waiting for transfers between devices, shards(): lax.psum_scatter(summed[0], 'col', scatter_dimension=0, tiled=True)  152 us
    psum x1, waiting for transfers between devices, shards(): summed = lax.psum((grad_term, curv_term), 'row')  94.6 us
    all_gather x1, blocking collectives, shards(): lax.all_gather(direction_raw, 'col', axis=0, tiled=True)  72.3 us
    all_gather x1, blocking collectives, shards(): lax.all_gather(weight_raw, 'col', axis=0, tiled=True)  65.7 us
  transfers between devices with their start and end apart: 4, of which 4 were waited for; matrix products, arithmetic and copies ran while one was open for 1% of the time, Pallas kernels for 0%

commit v1 on v0

v1 whole, which is shorter than its diff:
```python
import math

import jax
import jax.numpy as jnp
from jax import lax
from jax.sharding import PartitionSpec as P

ROUND_ROWS = 32


def symmetric(matrix):
    as_float = matrix.astype(jnp.float32)
    return ((as_float + as_float.T) * 0.5).astype(jnp.bfloat16)


def exchange_rows(value, mask, axis_size):
    return lax.ppermute(value, "row", [(i, i ^ mask) for i in range(axis_size)])


def gather_panel(features, panel_index, extra_rows):
    n_col = lax.axis_size("col")
    me = lax.axis_index("col")
    col_count = features.shape[0]
    count = panel_index.shape[0]
    owner = panel_index // col_count
    place = lax.iota(jnp.int32, count)
    earlier = (owner[:, None] == owner[None, :]) & (place[None, :] < place[:, None])
    rank = jnp.sum(earlier.astype(jnp.int32), axis=1)
    rounds = jnp.max(rank) // ROUND_ROWS + 1

    def own_rows(step):
        slot = rank - step * ROUND_ROWS
        chosen = (lax.iota(jnp.int32, ROUND_ROWS)[:, None] == slot[None, :]) & (owner == me)[None, :]
        local = jnp.sum(jnp.where(chosen, (panel_index - me * col_count)[None, :], 0), axis=1)
        return jnp.take(features, jnp.clip(local, 0, col_count - 1), axis=0)

    def spread(rows):
        sent = jnp.broadcast_to(rows[None], (n_col,) + rows.shape)
        return lax.all_to_all(sent, "col", 0, 0, tiled=True)

    def in_order(step, received):
        slot = rank - step * ROUND_ROWS
        wanted = jnp.where((slot >= 0) & (slot < ROUND_ROWS), owner * ROUND_ROWS + slot, -1)
        pick = (wanted[:, None] == lax.iota(jnp.int32, n_col * ROUND_ROWS)[None, :]).astype(jnp.bfloat16)
        flat = received.reshape(n_col * ROUND_ROWS, received.shape[-1])
        return jnp.dot(pick, flat, preferred_element_type=jnp.float32).astype(jnp.bfloat16)

    received = spread(jnp.concatenate([own_rows(0), extra_rows], axis=0))
    panel = in_order(0, received[:, :ROUND_ROWS])

    def another(state):
        step, rows = state
        return step + 1, rows + in_order(step, spread(own_rows(step)))

    _, panel = lax.while_loop(lambda state: state[0] < rounds, another, (jnp.int32(1), panel))
    return panel, received[:, ROUND_ROWS:]


def shards(features, weight_raw, direction_raw, panel_index, labels):
    n_row, n_col = lax.axis_size("row"), lax.axis_size("col")
    share = weight_raw.shape[0]
    dim = features.shape[1]
    col_count = features.shape[0]
    panel_count = panel_index.shape[0]
    panel_rows, matrices = gather_panel(
        features, panel_index, jnp.concatenate([weight_raw, direction_raw], axis=0)
    )
    weight_sym = symmetric(matrices[:, :share].reshape(dim, dim))
    direction_sym = symmetric(matrices[:, share:].reshape(dim, dim))
    proj_weight = jnp.dot(panel_rows, weight_sym, preferred_element_type=jnp.float32)
    proj_direction = jnp.dot(panel_rows, direction_sym, preferred_element_type=jnp.float32)
    projected = jnp.concatenate([proj_weight, proj_direction], axis=0).astype(jnp.bfloat16)
    pair_vals = lax.dot_general(
        projected, features, (((1,), (1,)), ((), ())), preferred_element_type=jnp.float32
    )
    margin = pair_vals[:panel_count]
    change = pair_vals[panel_count:]
    probability = jax.nn.sigmoid(margin)
    residual_weight = probability - labels.astype(jnp.float32)
    curvature_weight = probability * (1.0 - probability) * change
    pair_weights = jnp.concatenate([residual_weight, curvature_weight], axis=0).astype(jnp.bfloat16)
    col_sums = jnp.dot(pair_weights, features, preferred_element_type=jnp.float32)
    panel_float = panel_rows.astype(jnp.float32)
    pair_scale = 1.0 / math.sqrt(panel_count * n_row * col_count * n_col)
    highest = lax.Precision.HIGHEST
    grad_half = jnp.dot(
        panel_float.T, col_sums[:panel_count], preferred_element_type=jnp.float32, precision=highest
    )
    curv_half = jnp.dot(
        panel_float.T, col_sums[panel_count:], preferred_element_type=jnp.float32, precision=highest
    )
    grad_term = (grad_half + grad_half.T) * (0.5 * pair_scale)
    curv_term = (curv_half + curv_half.T) * (0.5 * pair_scale)
    first_core = lax.axis_index("row") % 2 == 0
    kept = jnp.where(first_core, grad_term, curv_term)
    given = jnp.where(first_core, curv_term, grad_term).astype(jnp.bfloat16)
    chip_sum = (kept + exchange_rows(given, 1, n_row).astype(jnp.float32)).astype(jnp.bfloat16)
    parts = lax.all_to_all(chip_sum.reshape(n_col, dim // n_col, dim), "col", 0, 0, tiled=True)
    mine = jnp.sum(parts.astype(jnp.float32), axis=0)
    near = mine + exchange_rows(mine, 2, n_row)
    far = exchange_rows(mine, 4, n_row) + exchange_rows(mine, 6, n_row)
    total = near + far
    other = exchange_rows(total, 1, n_row)
    gradient = jnp.where(first_core, total, other)
    hess_vec = jnp.where(first_core, other, total)
    return (gradient, hess_vec)


def solution(mesh):
    return jax.shard_map(
        shards,
        mesh=mesh,
        in_specs=(P("col", None), P("col", None), P("col", None), P("row"), P("row", "col")),
        out_specs=(P("col", None), P("col", None)),
        check_vma=False,
    )
```

time: 746 us -> 104 us (0.14)
  waiting for transfers between devices: 562 us -> 30.7 us
  blocking collectives: 138 us -> 15.1 us
  starting transfers between devices: 0.16 us -> 24 us
  between operations: 13.9 us -> 3.54 us
    reduce_scatter x2 -> x0, waiting for transfers between devices: 314 us -> none  [the longest x1 162 us: shards(): lax.psum_scatter(summed[1], 'col', scatter_dimension=0, tiled=True)]
    psum x2 -> x0, waiting for transfers between devices: 248 us -> none  [the longest x1 154 us: shards(): panel_rows = lax.psum(picked.astype(jnp.bfloat16), 'col')]
    all_gather x2 -> x0, blocking collectives: 138 us -> none  [the longest x1 72.3 us: shards(): lax.all_gather(direction_raw, 'col', axis=0, tiled=True)]
    all_to_all x0 -> x1, waiting for transfers between devices: none -> 23.6 us  [spread(): return lax.all_to_all(sent, 'col', 0, 0, tiled=True)]
    all_to_all x0 -> x1, blocking collectives: none -> 15.1 us  [shards(): lax.all_to_all(chip_sum.reshape(n_col, dim // n_col, dim), 'col', 0, 0, t...]
    ppermute x0 -> x5, starting transfers between devices: none -> 14.8 us  [exchange_rows(): return lax.ppermute(value, 'row', [(i, i ^ mask) for i in range(axis_size)])]
    all_to_all x0 -> x1, starting transfers between devices: none -> 9.22 us  [spread(): return lax.all_to_all(sent, 'col', 0, 0, tiled=True)]
  transfers between devices with their start and end apart: 4 -> 6, of which waited for: 4 -> 4; matrix products, arithmetic and copies ran while one was open for 1% -> 1% of each run, Pallas kernels for 0% -> 0%
where the time goes in v1:
time: 104 us
  waiting for transfers between devices  30.7 us (30%)
  starting transfers between devices  24 us (23%)
  blocking collectives  15.1 us (15%)
  local copies, waits for them, and re-layouts  10.8 us (10%)
  matrix products  10.8 us (10%)
  other arithmetic  8.51 us (8%)
  between operations  3.54 us (3%)
    all_to_all x1, waiting for transfers between devices, spread(): return lax.all_to_all(sent, 'col', 0, 0, tiled=True)  23.6 us
    all_to_all x1, blocking collectives, shards(): lax.all_to_all(chip_sum.reshape(n_col, dim // n_col, dim), 'col', 0, 0, t...  15.1 us
    ppermute x5, starting transfers between devices, exchange_rows(): return lax.ppermute(value, 'row', [(i, i ^ mask) for i in range(axis_size)])  14.8 us
    all_to_all x1, starting transfers between devices, spread(): return lax.all_to_all(sent, 'col', 0, 0, tiled=True)  9.22 us
    ppermute x5, waiting for transfers between devices, exchange_rows(): return lax.ppermute(value, 'row', [(i, i ^ mask) for i in range(axis_size)])  7.08 us
    convert_element_type x2, local copies, waits for them, and re-layouts, symmetric(): as_float = matrix.astype(jnp.float32)  2.67 us
    gather x1, local copies, waits for them, and re-layouts, own_rows(): return jnp.take(features, jnp.clip(local, 0, col_count - 1), axis=0)  2.49 us
    unnamed x14, local copies, waits for them, and re-layouts  2.39 us
  transfers between devices with their start and end apart: 6, of which 4 were waited for; matrix products, arithmetic and copies ran while one was open for 1% of the time, Pallas kernels for 0%

profile of v1, /device:TPU:1, one launch (start us, length us, event | category | flops | bytes accessed | tf_op | source)
XLA Modules:
  0.0 103.6 jit_solution(16380771086755433751)
XLA Ops:
  0.6 0.7 broadcast_compare_fusion.1
  1.3 0.7 broadcast_subtract_fusion.2
  2.4 2.5 %gather_fusion.1 = bf16[32,512]{1,0:T(8,128)(2,1)S(1)} fusion(bf16[2048,512]{1,0:T(8,128)(2,1)} %param.7, s32[1024]{0:T(1024)S(1)} %pad_clamp_fusion.1), kind=kCustom, calls=%fused_computation.1 | custom fusion | bytes 65664 | tf_op jit(solution)/shard_map/jit(_take)/gather | solution.py:35
  5.0 0.7 pad_maximum_fusion
  5.7 1.6 %broadcast_in_dim.87 = bf16[32,64,512]{2,1,0:T(8,128)(2,1)} broadcast(bf16[64,512]{1,0:T(8,128)(2,1)S(1)} %pad_maximum_fusion), dimensions={1,2} | broadcast | bytes 2162688 | tf_op jit(solution)/shard_map/broadcast_in_dim | solution.py:38
  7.3 9.2 %all-to-all-start.1 = ((bf16[32,64,512]{2,1,0:T(8,128)(2,1)}), bf16[32,64,512]{2,1,0:T(8,128)(2,1)S(1)}, u32[]{:S(2)}, u32[]{:S(2)}) async-start(bf16[32,64,512]{2,1,0:T(8,128)(2,1)} %broadcast_in_dim.87), calls=%async_computation.1 | async-start | bytes 4194304 | tf_op jit(solution)/shard_map/all_to_all | solution.py:39
  16.6 0.7 fusion.46
  20.0 23.6 %all-to-all-done.1 = bf16[32,64,512]{2,1,0:T(8,128)(2,1)S(1)} async-done(((bf16[32,64,512]{2,1,0:T(8,128)(2,1)}), bf16[32,64,512]{2,1,0:T(8,128)(2,1)S(1)}, u32[]{:S(2)}, u32[]{:S(2)}) %all-to-all-start.1) | async-done | bytes 2097184 | tf_op jit(solution)/shard_map/all_to_all | solution.py:39
  43.7 1.2 %copy-done.1 = bf16[32,64,512]{2,1,0:T(8,128)(2,1)} copy-done((bf16[32,64,512]{2,1,0:T(8,128)(2,1)}, bf16[32,64,512]{2,1,0:T(8,128)(2,1)S(1)}, u32[]{:S(2)}) %copy-start.1) | copy-done | bytes 2097176
  45.3 1.3 %copy.12 = f32[512,512]{0,1:T(8,128)} copy(f32[512,512]{1,0:T(8,128)S(1)} %get-tuple-element.115) | data formatting | bytes 2097152 | tf_op jit(solution)/shard_map/convert_element_type | solution.py:12
  46.7 1.3 %copy.11 = f32[512,512]{0,1:T(8,128)} copy(f32[512,512]{1,0:T(8,128)S(1)} %get-tuple-element.116) | data formatting | bytes 2097152 | tf_op jit(solution)/shard_map/convert_element_type | solution.py:12
  48.0 1.6 %fusion.16 = bf16[512,512]{1,0:T(8,128)(2,1)} fusion(bf16[1024,512]{1,0:T(8,128)(2,1)S(1)} %bitcast.64, s32[512]{0:T(512)S(1)} %get-tuple-element.114), kind=kOutput, calls=%fused_computation.34 | convolution fusion | flops 537657344 | bytes 1574912 | tf_op jit(solution)/shard_map/dot_general | solution.py:46
  49.6 2.0 %convolution_convert_fusion = bf16[512,512]{1,0:T(8,128)(2,1)S(1)} fusion(bf16[512,512]{1,0:T(8,128)(2,1)} %get-tuple-element.83, f32[512,512]{1,0:T(8,128)S(1)} %get-tuple-element.115, f32[512,512]{0,1:T(8,128)} %copy.12), kind=kOutput, calls=%fused_computation.35 | convolution fusion | flops 269484032 | bytes 3145728 | tf_op jit(solution)/shard_map/dot_general | solution.py:71
  52.0 1.1 %copy-done.5 = bf16[2048,512]{1,0:T(8,128)(2,1)S(1)} copy-done((bf16[2048,512]{1,0:T(8,128)(2,1)S(1)}, bf16[2048,512]{1,0:T(8,128)(2,1)}, u32[]{:S(2)}) %copy-start.5) | copy-done | bytes 2097176
  53.1 2.4 %fusion.21 = f32[1024,2048]{1,0:T(8,128)S(1)} fusion(bf16[2048,512]{1,0:T(8,128)(2,1)S(1)} %copy-done.5, bf16[512,512]{1,0:T(8,128)(2,1)S(1)} %convolution_convert_fusion, bf16[512,512]{1,0:T(8,128)(2,1)S(1)} %convolution_convert_fusion.1), kind=kOutput, calls=%fused_computation.41 | convolution fusion | flops 2149580800 | bytes 11534336 | tf_op jit(solution)/shard_map/dot_general | solution.py:73
  55.5 1.7 %subtract_convert_fusion = (bf16[512,2048]{1,0:T(8,128)(2,1)S(1)}, bf16[512,2048]{1,0:T(8,128)(2,1)S(1)}) fusion(s32[512,2048]{1,0:T(8,128)S(1)} %copy-done.4, f32[1024,2048]{1,0:T(8,128)S(1)} %fusion.21), kind=kLoop, calls=%fused_computation.31 | loop fusion | flops 10485760 | bytes 16777216 | tf_op jit(solution)/shard_map/convert.2
  57.3 2.3 %fusion.11 = f32[1024,512]{1,0:T(8,128)S(1)} fusion(bf16[2048,512]{1,0:T(8,128)(2,1)S(1)} %copy-done.5, bf16[512,2048]{1,0:T(8,128)(2,1)S(1)} %get-tuple-element.108, bf16[512,2048]{1,0:T(8,128)(2,1)S(1)} %get-tuple-element.107), kind=kOutput, calls=%fused_computation.27 | convolution fusion | flops 2155872256 | bytes 8388608 | tf_op jit(solution)/shard_map/dot_general | solution.py:82
  59.6 1.1 %fusion.17 = f32[512,512]{1,0:T(8,128)S(1)} fusion(bf16[512,512]{1,0:T(8,128)(2,1)S(1)} %copy-done.2, f32[1024,512]{1,0:T(8,128)S(1)} %fusion.11), kind=kOutput, calls=%fused_computation.37 | convolution fusion | flops 1610612736 | bytes 2621440 | tf_op jit(solution)/shard_map/dot_general | solution.py:89
  60.7 1.1 %fusion.19 = f32[512,512]{1,0:T(8,128)S(1)} fusion(bf16[512,512]{1,0:T(8,128)(2,1)S(1)} %copy-done.2, f32[1024,512]{1,0:T(8,128)S(1)} %fusion.11), kind=kOutput, calls=%fused_computation.39 | convolution fusion | flops 1610612736 | bytes 2621440 | tf_op jit(solution)/shard_map/dot_general | solution.py:86
  62.1 1.3 %copy.14 = f32[512,512]{0,1:T(8,128)} copy(f32[512,512]{1,0:T(8,128)S(1)} %fusion.17) | data formatting | bytes 2097152 | tf_op jit(solution)/shard_map/dot_general | solution.py:89
  63.4 1.8 %select_convert_fusion = bf16[512,512]{1,0:T(8,128)(2,1)S(1)} fusion(pred[]{:T(512)S(6)} %eq.93, f32[512,512]{1,0:T(8,128)S(1)} %fusion.19, f32[512,512]{0,1:T(8,128)S(1)} %copy.13, f32[512,512]{1,0:T(8,128)S(1)} %fusion.17, f32[512,512]{0,1:T(8,128)} %copy.14), kind=kLoop, calls=%fused_computation.57 | loop fusion | flops 1572864 | bytes 4718593 | tf_op jit(solution)/shard_map/convert_element_type | solution.py:96
  65.3 3.9 %collective-permute-start = (bf16[512,512]{1,0:T(8,128)(2,1)S(1)}, bf16[512,512]{1,0:T(8,128)(2,1)S(1)}, u32[]{:S(2)}, u32[]{:S(2)}) collective-permute-start(bf16[512,512]{1,0:T(8,128)(2,1)S(1)} %select_convert_fusion), channel_id=1, source_target_pairs={{0,32},{32,0},{64,96},{96,64},{128,160},{160,128},{192,224},{224,1... | collective-permute-start | bytes 1572872 | tf_op jit(solution)/shard_map/ppermute | solution.py:17
  69.2 1.5 %collective-permute-done = bf16[512,512]{1,0:T(8,128)(2,1)S(1)} collective-permute-done((bf16[512,512]{1,0:T(8,128)(2,1)S(1)}, bf16[512,512]{1,0:T(8,128)(2,1)S(1)}, u32[]{:S(2)}, u32[]{:S(2)}) %collective-permute-start) | collective-permute-done | bytes 524320 | tf_op jit(solution)/shard_map/ppermute | solution.py:17
  70.7 0.6 add_convert_fusion
  71.3 15.1 %all_to_all.17 = bf16[32,16,512]{2,1,0:T(8,128)(2,1)S(1)} all-to-all(bf16[32,16,512]{2,1,0:T(8,128)(2,1)S(1)} %bitcast.65), channel_id=1, replica_groups=mesh['row'=8,'col'=32] {'col'}, dimensions={0} | all-to-all | bytes 1048576 | tf_op jit(solution)/shard_map/all_to_all | solution.py:98
  86.5 5.2 %collective-permute-start.3 = (f32[16,512]{1,0:T(8,128)S(1)}, f32[16,512]{1,0:T(8,128)S(1)}, u32[]{:S(2)}, u32[]{:S(2)}) collective-permute-start(f32[16,512]{1,0:T(8,128)S(1)} %convert_reduce_fusion), channel_id=1, source_target_pairs={{0,192},{32,224},{64,128},{96,160},{128,64},{160,96},{192,0},{224,... | collective-permute-start | bytes 98312 | tf_op jit(solution)/shard_map/ppermute | solution.py:17
  91.7 1.2 %collective-permute-start.2 = (f32[16,512]{1,0:T(8,128)S(1)}, f32[16,512]{1,0:T(8,128)S(1)}, u32[]{:S(2)}, u32[]{:S(2)}) collective-permute-start(f32[16,512]{1,0:T(8,128)S(1)} %convert_reduce_fusion), channel_id=1, source_target_pairs={{0,128},{32,160},{64,192},{96,224},{128,0},{160,32},{192,64},{224,... | collective-permute-start | bytes 98312 | tf_op jit(solution)/shard_map/ppermute | solution.py:17
  92.8 1.0 collective-permute-start.1
  93.9 4.7 %collective-permute-done.2 = f32[16,512]{1,0:T(8,128)S(1)} collective-permute-done((f32[16,512]{1,0:T(8,128)S(1)}, f32[16,512]{1,0:T(8,128)S(1)}, u32[]{:S(2)}, u32[]{:S(2)}) %collective-permute-start.2) | collective-permute-done | bytes 32800 | tf_op jit(solution)/shard_map/ppermute | solution.py:17
  98.6 3.5 %collective-permute-start.4 = (f32[16,512]{1,0:T(8,128)S(1)}, f32[16,512]{1,0:T(8,128)S(1)}, u32[]{:S(2)}, u32[]{:S(2)}) collective-permute-start(f32[16,512]{1,0:T(8,128)S(1)} %add_add_fusion), channel_id=1, source_target_pairs={{0,32},{32,0},{64,96},{96,64},{128,160},{160,128},{192,224},{224,1... | collective-permute-start | bytes 98312 | tf_op jit(solution)/shard_map/ppermute | solution.py:17
  102.1 0.9 collective-permute-done.4
  102.9 0.6 broadcast_select_fusion.2
  (29 shorter events, 1.8 us)
Async XLA Ops:
  7.3 36.3 %all-to-all-start.1 = ((bf16[32,64,512]{2,1,0:T(8,128)(2,1)}), bf16[32,64,512]{2,1,0:T(8,128)(2,1)S(1)}, u32[]{:S(2)}, u32[]{:S(2)}) async-start(bf16[32,64,512]{2,1,0:T(8,128)(2,1)} %broadcast_in_dim.87), calls=%async_computation.1 | async-start | bytes 4194304 | tf_op jit(solution)/shard_map/all_to_all | solution.py:39
  43.6 1.3 %copy-start.1 = (bf16[32,64,512]{2,1,0:T(8,128)(2,1)}, bf16[32,64,512]{2,1,0:T(8,128)(2,1)S(1)}, u32[]{:S(2)}) copy-start(bf16[32,64,512]{2,1,0:T(8,128)(2,1)S(1)} %all-to-all-done.1) | copy-start | bytes 6291460
  46.7 1.3 %slice-start = ((bf16[32,64,512]{2,1,0:T(8,128)(2,1)}), bf16[32,32,512]{2,1,0:T(8,128)(2,1)S(1)}, s32[]{:S(2)}) async-start(bf16[32,64,512]{2,1,0:T(8,128)(2,1)} %copy-done.1), calls=%async_computation.3 | async-start | bytes 2097152 | tf_op jit(solution)/shard_map/slice | solution.py:49
  48.0 1.6 %copy-start.6 = (s32[512]{0:T(512)S(1)}, s32[512]{0:T(512)}, u32[]{:S(2)}) copy-start(s32[512]{0:T(512)} %param.10) | copy-start | bytes 6148
  49.6 2.0 %copy-start.2 = (bf16[512,512]{1,0:T(8,128)(2,1)S(1)}, bf16[512,512]{1,0:T(8,128)(2,1)}, u32[]{:S(2)}) copy-start(bf16[512,512]{1,0:T(8,128)(2,1)} %get-tuple-element.83) | copy-start | bytes 1572868
  49.6 2.0 %copy-start.3 = (f32[512,512]{0,1:T(8,128)S(1)}, f32[512,512]{0,1:T(8,128)}, u32[]{:S(2)}) copy-start(f32[512,512]{0,1:T(8,128)} %copy.11) | copy-start | bytes 3145732
  51.6 1.6 %copy-start.5 = (bf16[2048,512]{1,0:T(8,128)(2,1)S(1)}, bf16[2048,512]{1,0:T(8,128)(2,1)}, u32[]{:S(2)}) copy-start(bf16[2048,512]{1,0:T(8,128)(2,1)} %get-tuple-element.216) | copy-start | bytes 6291460
  53.1 2.4 %copy-start.4 = (s32[512,2048]{1,0:T(8,128)S(1)}, s32[512,2048]{1,0:T(8,128)}, u32[]{:S(2)}) copy-start(s32[512,2048]{1,0:T(8,128)} %param.11) | copy-start | bytes 12582916
  63.4 7.3 %copy-start = (f32[512,512]{0,1:T(8,128)S(1)}, f32[512,512]{0,1:T(8,128)}, u32[]{:S(2)}) copy-start(f32[512,512]{0,1:T(8,128)} %copy.14) | copy-start | bytes 3145732
  65.3 5.4 %collective-permute-start = (bf16[512,512]{1,0:T(8,128)(2,1)S(1)}, bf16[512,512]{1,0:T(8,128)(2,1)S(1)}, u32[]{:S(2)}, u32[]{:S(2)}) collective-permute-start(bf16[512,512]{1,0:T(8,128)(2,1)S(1)} %select_convert_fusion), channel_id=1, source_target_pairs={{0,32},{32,0},{64,96},{96,64},{128,160},{160,128},{192,224},{224,1... | collective-permute-start | bytes 1572872 | tf_op jit(solution)/shard_map/ppermute | solution.py:17
  86.5 7.4 %collective-permute-start.3 = (f32[16,512]{1,0:T(8,128)S(1)}, f32[16,512]{1,0:T(8,128)S(1)}, u32[]{:S(2)}, u32[]{:S(2)}) collective-permute-start(f32[16,512]{1,0:T(8,128)S(1)} %convert_reduce_fusion), channel_id=1, source_target_pairs={{0,192},{32,224},{64,128},{96,160},{128,64},{160,96},{192,0},{224,... | collective-permute-start | bytes 98312 | tf_op jit(solution)/shard_map/ppermute | solution.py:17
  91.7 6.9 %collective-permute-start.2 = (f32[16,512]{1,0:T(8,128)S(1)}, f32[16,512]{1,0:T(8,128)S(1)}, u32[]{:S(2)}, u32[]{:S(2)}) collective-permute-start(f32[16,512]{1,0:T(8,128)S(1)} %convert_reduce_fusion), channel_id=1, source_target_pairs={{0,128},{32,160},{64,192},{96,224},{128,0},{160,32},{192,64},{224,... | collective-permute-start | bytes 98312 | tf_op jit(solution)/shard_map/ppermute | solution.py:17
  92.8 5.7 %collective-permute-start.1 = (f32[16,512]{1,0:T(8,128)S(1)}, f32[16,512]{1,0:T(8,128)S(1)}, u32[]{:S(2)}, u32[]{:S(2)}) collective-permute-start(f32[16,512]{1,0:T(8,128)S(1)} %convert_reduce_fusion), channel_id=1, source_target_pairs={{0,64},{32,96},{64,0},{96,32},{128,192},{160,224},{192,128},{224,1... | collective-permute-start | bytes 98312 | tf_op jit(solution)/shard_map/ppermute | solution.py:17
  98.6 4.4 %collective-permute-start.4 = (f32[16,512]{1,0:T(8,128)S(1)}, f32[16,512]{1,0:T(8,128)S(1)}, u32[]{:S(2)}, u32[]{:S(2)}) collective-permute-start(f32[16,512]{1,0:T(8,128)S(1)} %add_add_fusion), channel_id=1, source_target_pairs={{0,32},{32,0},{64,96},{96,64},{128,160},{160,128},{192,224},{224,1... | collective-permute-start | bytes 98312 | tf_op jit(solution)/shard_map/ppermute | solution.py:17

commit v2 on v0

v2 whole, which is shorter than its diff:
```python
import functools
import math

import jax
import jax.numpy as jnp
from jax import lax
from jax.experimental import pallas as pl
from jax.experimental.pallas import tpu as pltpu
from jax.sharding import PartitionSpec as P

BF16, F32, I32 = jnp.bfloat16, jnp.float32, jnp.int32
ROUND_ROWS = 32
STEP_ROWS = 256

in_vmem = functools.partial(pl.BlockSpec, memory_space=pltpu.VMEM)
in_smem = functools.partial(pl.BlockSpec, memory_space=pltpu.SMEM)
in_place = functools.partial(pl.BlockSpec, memory_space=pl.ANY)
params = functools.partial(pltpu.CompilerParams, vmem_limit_bytes=48 << 20)


def rows_of(a, b):
    return jnp.dot(a, b, preferred_element_type=F32)


def exchange(value, mask):
    return lax.ppermute(value, "row", [(i, i ^ mask) for i in range(lax.axis_size("row"))])


def pack_rows(features, panel_row, extra_rows, step):
    n_col = lax.axis_size("col")
    col_count, dim = features.shape
    count = panel_row.shape[1]
    n_extra = 0 if extra_rows is None else extra_rows[0].shape[0]

    def body(step_ref, panel_ref, *refs):
        extra, (features_hbm, out, table, arrived) = refs[:-4], refs[-4:]
        load = pltpu.make_async_copy(features_hbm, table, arrived)
        load.start()
        place = jnp.broadcast_to(panel_ref[...], (8, count)) - lax.axis_index("col") * col_count
        owned = (place >= 0) & (place < col_count)
        lane = lax.broadcasted_iota(I32, (8, count), 1)
        running = owned.astype(I32)
        shift = 1
        while shift < count:
            running = running + jnp.where(lane >= shift, pltpu.roll(running, shift, axis=1), 0)
            shift *= 2
        slot = jnp.where(owned, running - 1 - step_ref[0] * ROUND_ROWS, -1)[:1]
        mine = slot == lax.broadcasted_iota(I32, (ROUND_ROWS, count), 0)
        wanted = jnp.sum(jnp.where(mine, place[:1] + 1, 0), axis=1, keepdims=True) - 1
        pick = (wanted == lax.broadcasted_iota(I32, (ROUND_ROWS, col_count), 1)).astype(F32).astype(BF16)
        load.wait()
        message = rows_of(pick, table[...]).astype(BF16)
        if extra:
            second = lax.axis_index("row") % 2 == 1
            mixed = jnp.where(second, extra[1][...].astype(F32), extra[0][...].astype(F32))
            message = jnp.concatenate([message, mixed.astype(BF16)], axis=0)
        for peer in range(n_col):
            out[peer] = message

    return pl.pallas_call(
        body,
        name="pack_rows",
        out_shape=jax.ShapeDtypeStruct((n_col, ROUND_ROWS + n_extra, dim), BF16),
        in_specs=[in_smem(), in_vmem()] + [in_vmem()] * (0 if extra_rows is None else 2) + [in_place()],
        out_specs=in_vmem(),
        scratch_shapes=[pltpu.VMEM((col_count, dim), BF16), pltpu.SemaphoreType.DMA(())],
        compiler_params=params(),
    )(step, panel_row, *(extra_rows or ()), features)


def rank_rows(panel_row, panel_column, col_count):
    count = panel_row.shape[1]
    bits = col_count.bit_length() - 1

    def body(row_ref, column_ref, where, rounds):
        owner_row = lax.shift_right_logical(row_ref[...], bits)
        owner = lax.shift_right_logical(column_ref[...], bits)
        before = lax.broadcasted_iota(I32, (count, count), 1) < lax.broadcasted_iota(I32, (count, count), 0)
        same = jnp.where(before & (owner == owner_row), 1, 0)
        rank = jnp.sum(same, axis=1, keepdims=True)
        lane = lax.broadcasted_iota(I32, (count, 128), 1)
        where[...] = jnp.where(lane == 0, owner, rank)
        rounds[0] = jnp.max(rank) // ROUND_ROWS + 1

    assert col_count == 1 << bits
    return pl.pallas_call(
        body,
        name="rank_rows",
        out_shape=(jax.ShapeDtypeStruct((count, 128), I32), jax.ShapeDtypeStruct((1,), I32)),
        in_specs=[in_vmem(), in_vmem()],
        out_specs=(in_vmem(), in_smem()),
        compiler_params=params(),
    )(panel_row, panel_column)


def ordered(where, received, step):
    n_col, _, dim = received.shape
    rank = where[:, 1:2] - step * ROUND_ROWS
    slot = jnp.where((rank >= 0) & (rank < ROUND_ROWS), where[:, :1] * ROUND_ROWS + rank, -1)
    pick = slot == lax.broadcasted_iota(I32, (where.shape[0], n_col * ROUND_ROWS), 1)
    return rows_of(pick.astype(F32).astype(BF16), received[:, :ROUND_ROWS, :].reshape(n_col * ROUND_ROWS, dim))


def add_round(where, received, panel, step):
    def body(step_ref, where_ref, received_ref, panel_ref, out):
        fresh = ordered(where_ref[...], received_ref[...], step_ref[0])
        out[...] = (panel_ref[...].astype(F32) + fresh).astype(BF16)

    return pl.pallas_call(
        body,
        name="add_round",
        out_shape=jax.ShapeDtypeStruct(panel.shape, BF16),
        in_specs=[in_smem(), in_vmem(), in_vmem(), in_vmem()],
        out_specs=in_vmem(),
        compiler_params=params(),
    )(step, where, received, panel)


def symmetric_matrix(received):
    dim = received.shape[2]

    def body(received_ref, out):
        raw = received_ref[:, ROUND_ROWS:, :].reshape(dim, dim).astype(F32)
        out[...] = ((raw + raw.T) * 0.5).astype(BF16)

    return pl.pallas_call(
        body,
        name="symmetric_matrix",
        out_shape=jax.ShapeDtypeStruct((dim, dim), BF16),
        in_specs=[in_vmem()],
        out_specs=in_vmem(),
        compiler_params=params(),
    )(received)


def pair_products(panel, kept_matrix, other_matrix, features, labels):
    count, dim = panel.shape
    col_count = features.shape[0]
    steps = count // STEP_ROWS

    def body(panel_ref, kept_ref, other_ref, features_ref, labels_hbm, kept, given, projected, sums, labels_ref, arrived):
        loads = []
        for i in range(steps):
            part = pl.ds(i * STEP_ROWS, STEP_ROWS)
            loads.append(pltpu.make_async_copy(labels_hbm.at[part], labels_ref.at[part], arrived.at[i]))
            loads[i].start()
        core = lax.axis_index("row") % 2
        rows = panel_ref[...]
        projected[core] = rows_of(rows, kept_ref[...]).astype(BF16)
        projected[1 - core] = rows_of(rows, other_ref[...]).astype(BF16)
        columns = features_ref[...]
        for i in range(steps):
            part = pl.ds(i * STEP_ROWS, STEP_ROWS)
            both = jnp.concatenate([projected[0, part], projected[1, part]], axis=0)
            pairs = lax.dot_general(both, columns, (((1,), (1,)), ((), ())), preferred_element_type=F32)
            loads[i].wait()
            probability = 1.0 / (1.0 + jnp.exp(-pairs[:STEP_ROWS]))
            residual = (probability - labels_ref[part].astype(F32)).astype(BF16)
            curvature = (probability * (1.0 - probability) * pairs[STEP_ROWS:]).astype(BF16)
            total = rows_of(jnp.concatenate([residual, curvature], axis=0), columns).astype(BF16)
            sums[0, part] = total[:STEP_ROWS]
            sums[1, part] = total[STEP_ROWS:]
        turned = rows.T
        for out, place in ((kept, core), (given, 1 - core)):
            half = rows_of(turned, sums[place])
            out[...] = (half + half.T).astype(out.dtype)

    return pl.pallas_call(
        body,
        name="pair_products",
        out_shape=(jax.ShapeDtypeStruct((dim, dim), F32), jax.ShapeDtypeStruct((dim, dim), BF16)),
        in_specs=[in_vmem()] * 4 + [in_place()],
        out_specs=(in_vmem(), in_vmem()),
        scratch_shapes=[
            pltpu.VMEM((2, count, dim), BF16),
            pltpu.VMEM((2, count, dim), BF16),
            pltpu.VMEM((count, col_count), I32),
            pltpu.SemaphoreType.DMA((steps,)),
        ],
        compiler_params=params(),
    )(panel, kept_matrix, other_matrix, features, labels)


def shards(features, weight_raw, direction_raw, panel_index, labels):
    n_row, n_col = lax.axis_size("row"), lax.axis_size("col")
    col_count, dim = features.shape
    count = panel_index.shape[0]
    panel_row = panel_index.reshape(1, count)
    first = jnp.zeros((1,), I32)
    sent = pack_rows(features, panel_row, (weight_raw, direction_raw), first)
    received = lax.all_to_all(sent, "col", 0, 0, tiled=True)
    where, rounds = rank_rows(panel_row, panel_index.reshape(count, 1), col_count)
    kept_matrix = symmetric_matrix(received)
    other_matrix = exchange(kept_matrix, 1)
    panel = add_round(where, received, jnp.zeros((count, dim), BF16), first)

    def another(state):
        step, rows = state
        fresh = lax.all_to_all(pack_rows(features, panel_row, None, step), "col", 0, 0, tiled=True)
        return step + 1, add_round(where, fresh, rows, step)

    _, panel = lax.while_loop(lambda state: state[0][0] < rounds[0], another, (first + 1, panel))
    kept, given = pair_products(panel, kept_matrix, other_matrix, features, labels)
    chip_sum = (kept + exchange(given, 1).astype(F32)).astype(BF16)
    parts = lax.all_to_all(chip_sum.reshape(n_col, dim // n_col, dim), "col", 0, 0, tiled=True)
    mine = jnp.sum(parts.astype(F32), axis=0)
    near = mine + exchange(mine, 2)
    scale = 0.5 / math.sqrt(count * n_row * col_count * n_col)
    total = (near + exchange(near, 6)) * scale
    other = exchange(total, 1)
    on_first = lax.axis_index("row") % 2 == 0
    return jnp.where(on_first, total, other), jnp.where(on_first, other, total)


def solution(mesh):
    return jax.shard_map(
        shards,
        mesh=mesh,
        in_specs=(P("col", None), P("col", None), P("col", None), P("row"), P("row", "col")),
        out_specs=(P("col", None), P("col", None)),
        check_vma=False,
    )
```

time: 746 us -> 81.5 us (0.11)
  waiting for transfers between devices: 562 us -> 5.72 us
  blocking collectives: 138 us -> 44.4 us
  starting transfers between devices: 0.16 us -> 13.9 us
  Pallas kernels: 0 us -> 13.2 us
  between operations: 13.9 us -> 0.75 us
  matrix products: 10.7 us -> 0 us
  local copies, waits for them, and re-layouts: 12 us -> 1.62 us
  other arithmetic: 8.43 us -> 0.89 us
    reduce_scatter x2 -> x0, waiting for transfers between devices: 314 us -> none  [the longest x1 162 us: shards(): lax.psum_scatter(summed[1], 'col', scatter_dimension=0, tiled=True)]
    psum x2 -> x0, waiting for transfers between devices: 248 us -> none  [the longest x1 154 us: shards(): panel_rows = lax.psum(picked.astype(jnp.bfloat16), 'col')]
    all_gather x2 -> x0, blocking collectives: 138 us -> none  [the longest x1 72.3 us: shards(): lax.all_gather(direction_raw, 'col', axis=0, tiled=True)]
    all_to_all x0 -> x2, blocking collectives: none -> 44.4 us  [the longest x1 30.2 us: shards(): received = lax.all_to_all(sent, 'col', 0, 0, tiled=True)]
    ppermute x0 -> x5, starting transfers between devices: none -> 13.9 us  [exchange(): lax.ppermute(value, 'row', [(i, i ^ mask) for i in range(lax.axis_size('r...]
    pallas_call x0 -> x5, Pallas kernels: none -> 13.2 us  [the longest x1 8.18 us: pair_products(): pl.pallas_call(body, name='pair_products', out_shape=(jax.ShapeDtypeStruc...]
    dot_general x6 -> x0, matrix products: 10.7 us -> none  [the longest x1 2.46 us: shards(): jnp.dot(panel_float.T, curv_sums, preferred_element_type=jnp.float32, pre...]
  transfers between devices with their start and end apart: 4 -> 5, of which waited for: 4 -> 4; matrix products, arithmetic and copies ran while one was open for 1% -> 0% of each run, Pallas kernels for 0% -> 2%
where the time goes in v2:
time: 81.5 us; the launch traced here: 81.1 us
  blocking collectives  44.4 us (54%)
  starting transfers between devices  13.9 us (17%)
  Pallas kernels  13.2 us (16%)
  waiting for transfers between devices  5.72 us (7%)
  local copies, waits for them, and re-layouts  1.62 us (2%)
  other arithmetic  0.89 us (1%)
    all_to_all x1, blocking collectives, shards(): received = lax.all_to_all(sent, 'col', 0, 0, tiled=True)  30.2 us
    all_to_all x1, blocking collectives, shards(): lax.all_to_all(chip_sum.reshape(n_col, dim // n_col, dim), 'col', 0, 0, t...  14.3 us
    ppermute x5, starting transfers between devices, exchange(): lax.ppermute(value, 'row', [(i, i ^ mask) for i in range(lax.axis_size('r...  13.9 us
    pallas_call x1, Pallas kernels, pair_products(): pl.pallas_call(body, name='pair_products', out_shape=(jax.ShapeDtypeStruc...  8.18 us
    ppermute x5, waiting for transfers between devices, exchange(): lax.ppermute(value, 'row', [(i, i ^ mask) for i in range(lax.axis_size('r...  5.72 us
    pallas_call x1, Pallas kernels, pack_rows(): pl.pallas_call(body, name='pack_rows', out_shape=jax.ShapeDtypeStruct((n_...  2.88 us
  transfers between devices with their start and end apart: 5, of which 4 were waited for; matrix products, arithmetic and copies ran while one was open for 0% of the time, Pallas kernels for 2%

profile of v2, /device:TPU:1, one launch (start us, length us, event | category | flops | bytes accessed | tf_op | source)
XLA Modules:
  0.0 81.1 jit_solution(60876347013145662)
XLA Ops:
  0.6 0.0 copy-start
  0.6 0.7 copy-done
  1.3 0.0 copy-start.1
  1.4 0.7 copy-done.1
  2.1 2.9 %pack_rows.2 = bf16[32,48,512]{2,1,0:T(8,128)(2,1)S(1)} custom-call(s32[1]{0:T(128)} %constant.28.clone.1.step_ref, s32[1,512]{1,0:T(1,128)} %bitcast.6, bf16[16,512]{1,0:T(8,128)(2,1)S(1)} %copy-done, bf16[16,512]{1,0:T(8,128)(2,1)S(1)} %copy-done.1, bf16[2048,512]{1,0:T(8,128)(2,1)} %features_ref.1), custom_call_target="tpu_custom_call" | custom-call | tf_op jit(solution)/shard_map/pack_rows/pallas_call | solution.py:60
  5.0 0.0 copy-start.4
  5.0 30.2 %all_to_all.15.received_ref = bf16[32,48,512]{2,1,0:T(8,128)(2,1)S(1)} all-to-all(bf16[32,48,512]{2,1,0:T(8,128)(2,1)S(1)} %pack_rows.2), channel_id=1, replica_groups=mesh['row'=8,'col'=32] {'col'}, dimensions={0} | all-to-all | bytes 3145728 | tf_op jit(solution)/shard_map/all_to_all | solution.py:191
  35.1 0.2 symmetric_matrix.1.kept_ref
  35.4 2.7 %collective-permute-start = (bf16[512,512]{1,0:T(8,128)(2,1)S(1)}, bf16[512,512]{1,0:T(8,128)(2,1)S(1)}, u32[]{:S(2)}, u32[]{:S(2)}) collective-permute-start(bf16[512,512]{1,0:T(8,128)(2,1)S(1)} %symmetric_matrix.1.kept_ref), channel_id=1, source_target_pairs={{0,32},{32,0},{64,96},{96,64},{128,160},{160,128},{192,224},{224,1... | collective-permute-start | bytes 1572872 | tf_op jit(solution)/shard_map/ppermute | solution.py:26
  38.0 0.0 copy-done.4
  38.0 0.1 copy.7.column_ref
  38.2 0.0 copy-start.2
  38.2 0.9 %rank_rows.1 = (s32[512,128]{1,0:T(8,128)S(1)}, s32[1]{0:T(128)}) custom-call(s32[1,512]{1,0:T(1,128)S(1)} %bitcast.8, s32[512,1]{1,0:T(8,128)S(1)} %copy.7.column_ref), custom_call_target="tpu_custom_call" | custom-call | tf_op jit(solution)/shard_map/rank_rows/pallas_call | solution.py:86
  39.1 1.0 %add_round.2 = bf16[512,512]{1,0:T(8,128)(2,1)S(1)} custom-call(s32[1]{0:T(128)} %constant.28.clone.1.step_ref, s32[512,128]{1,0:T(8,128)S(1)} %get-tuple-element.95.where_ref, bf16[32,48,512]{2,1,0:T(8,128)(2,1)S(1)} %all_to_all.15.received_ref, bf16[512,512]{1,0:T(8,128)(2,1)S(1)} %broadcast_in_dim.3.panel_ref), custom_call_target="tpu_custom_call" | custom-call | tf_op jit(solution)/shard_map/add_round/pallas_call | solution.py:109
  40.1 0.0 copy-done.2
  40.1 0.7 while.10
  40.8 0.0 collective-permute-done.other_ref
  40.8 8.2 %pair_products.1 = (f32[512,512]{1,0:T(8,128)S(1)}, bf16[512,512]{1,0:T(8,128)(2,1)S(1)}) custom-call(bf16[512,512]{1,0:T(8,128)(2,1)S(1)} %get-tuple-element.116, bf16[512,512]{1,0:T(8,128)(2,1)S(1)} %symmetric_matrix.1.kept_ref, bf16[512,512]{1,0:T(8,128)(2,1)S(1)} %collective-permute-done.other_ref, bf16[2048,512]{1,0:T(8,128)(2,1)} %features_ref.1, ...), custom_call_target="tpu_custom_call" | custom-call | tf_op jit(solution)/shard_map/pair_products/pallas_call | solution.py:168
  49.0 0.1 collective-permute-start.1
  49.1 1.9 %collective-permute-done.1 = bf16[512,512]{1,0:T(8,128)(2,1)S(1)} collective-permute-done((bf16[512,512]{1,0:T(8,128)(2,1)S(1)}, bf16[512,512]{1,0:T(8,128)(2,1)S(1)}, u32[]{:S(2)}, u32[]{:S(2)}) %collective-permute-start.1) | collective-permute-done | bytes 524320 | tf_op jit(solution)/shard_map/ppermute | solution.py:26
  51.0 0.2 add_convert_fusion
  51.2 14.3 %all_to_all.16 = bf16[32,16,512]{2,1,0:T(8,128)(2,1)S(1)} all-to-all(bf16[32,16,512]{2,1,0:T(8,128)(2,1)S(1)} %bitcast.5), channel_id=1, replica_groups=mesh['row'=8,'col'=32] {'col'}, dimensions={0} | all-to-all | bytes 1048576 | tf_op jit(solution)/shard_map/all_to_all | solution.py:205
  65.4 0.1 convert_reduce_fusion
  65.5 3.1 %collective-permute-start.2 = (f32[16,512]{1,0:T(8,128)S(1)}, f32[16,512]{1,0:T(8,128)S(1)}, u32[]{:S(2)}, u32[]{:S(2)}) collective-permute-start(f32[16,512]{1,0:T(8,128)S(1)} %convert_reduce_fusion), channel_id=1, source_target_pairs={{0,64},{32,96},{64,0},{96,32},{128,192},{160,224},{192,128},{224,1... | collective-permute-start | bytes 98312 | tf_op jit(solution)/shard_map/ppermute | solution.py:26
  68.6 1.7 %collective-permute-done.2 = f32[16,512]{1,0:T(8,128)S(1)} collective-permute-done((f32[16,512]{1,0:T(8,128)S(1)}, f32[16,512]{1,0:T(8,128)S(1)}, u32[]{:S(2)}, u32[]{:S(2)}) %collective-permute-start.2) | collective-permute-done | bytes 32800 | tf_op jit(solution)/shard_map/ppermute | solution.py:26
  70.3 4.1 %collective-permute-start.3 = (f32[16,512]{1,0:T(8,128)S(1)}, f32[16,512]{1,0:T(8,128)S(1)}, u32[]{:S(2)}, u32[]{:S(2)}) collective-permute-start(f32[16,512]{1,0:T(8,128)S(1)} %add.18), channel_id=1, source_target_pairs={{0,192},{32,224},{64,128},{96,160},{128,64},{160,96},{192,0},{224,... | collective-permute-start | bytes 98312 | tf_op jit(solution)/shard_map/ppermute | solution.py:26
  74.4 1.3 %collective-permute-done.3 = f32[16,512]{1,0:T(8,128)S(1)} collective-permute-done((f32[16,512]{1,0:T(8,128)S(1)}, f32[16,512]{1,0:T(8,128)S(1)}, u32[]{:S(2)}, u32[]{:S(2)}) %collective-permute-start.3) | collective-permute-done | bytes 32800 | tf_op jit(solution)/shard_map/ppermute | solution.py:26
  75.7 3.9 %collective-permute-start.4 = (f32[16,512]{1,0:T(8,128)S(1)}, f32[16,512]{1,0:T(8,128)S(1)}, u32[]{:S(2)}, u32[]{:S(2)}) collective-permute-start(f32[16,512]{1,0:T(8,128)S(1)} %add_multiply_fusion), channel_id=1, source_target_pairs={{0,32},{32,0},{64,96},{96,64},{128,160},{160,128},{192,224},{224,1... | collective-permute-start | bytes 98312 | tf_op jit(solution)/shard_map/ppermute | solution.py:26
  79.7 0.9 %collective-permute-done.4 = f32[16,512]{1,0:T(8,128)S(1)} collective-permute-done((f32[16,512]{1,0:T(8,128)S(1)}, f32[16,512]{1,0:T(8,128)S(1)}, u32[]{:S(2)}, u32[]{:S(2)}) %collective-permute-start.4) | collective-permute-done | bytes 32800 | tf_op jit(solution)/shard_map/ppermute | solution.py:26
  80.5 0.6 broadcast_select_fusion
  (3 shorter events, 0.1 us)
Async XLA Ops:
  0.6 0.7 copy-start
  1.3 0.7 copy-start.1
  5.0 33.1 %copy-start.4 = (s32[512]{0:T(512)S(1)}, s32[512]{0:T(512)}, u32[]{:S(2)}) copy-start(s32[512]{0:T(512)} %param.10) | copy-start | bytes 6148
  35.4 5.5 %collective-permute-start = (bf16[512,512]{1,0:T(8,128)(2,1)S(1)}, bf16[512,512]{1,0:T(8,128)(2,1)S(1)}, u32[]{:S(2)}, u32[]{:S(2)}) collective-permute-start(bf16[512,512]{1,0:T(8,128)(2,1)S(1)} %symmetric_matrix.1.kept_ref), channel_id=1, source_target_pairs={{0,32},{32,0},{64,96},{96,64},{128,160},{160,128},{192,224},{224,1... | collective-permute-start | bytes 1572872 | tf_op jit(solution)/shard_map/ppermute | solution.py:26
  38.2 1.9 %copy-start.2 = (bf16[2048,512]{1,0:T(8,128)(2,1)S(1)}, bf16[2048,512]{1,0:T(8,128)(2,1)}, u32[]{:S(2)}) copy-start(bf16[2048,512]{1,0:T(8,128)(2,1)} %features_ref.1) | copy-start | bytes 6291460
  49.0 2.0 %collective-permute-start.1 = (bf16[512,512]{1,0:T(8,128)(2,1)S(1)}, bf16[512,512]{1,0:T(8,128)(2,1)S(1)}, u32[]{:S(2)}, u32[]{:S(2)}) collective-permute-start(bf16[512,512]{1,0:T(8,128)(2,1)S(1)} %get-tuple-element.43), channel_id=1, source_target_pairs={{0,32},{32,0},{64,96},{96,64},{128,160},{160,128},{192,224},{224,1... | collective-permute-start | bytes 1572872 | tf_op jit(solution)/shard_map/ppermute | solution.py:26
  65.5 4.7 %collective-permute-start.2 = (f32[16,512]{1,0:T(8,128)S(1)}, f32[16,512]{1,0:T(8,128)S(1)}, u32[]{:S(2)}, u32[]{:S(2)}) collective-permute-start(f32[16,512]{1,0:T(8,128)S(1)} %convert_reduce_fusion), channel_id=1, source_target_pairs={{0,64},{32,96},{64,0},{96,32},{128,192},{160,224},{192,128},{224,1... | collective-permute-start | bytes 98312 | tf_op jit(solution)/shard_map/ppermute | solution.py:26
  70.3 5.4 %collective-permute-start.3 = (f32[16,512]{1,0:T(8,128)S(1)}, f32[16,512]{1,0:T(8,128)S(1)}, u32[]{:S(2)}, u32[]{:S(2)}) collective-permute-start(f32[16,512]{1,0:T(8,128)S(1)} %add.18), channel_id=1, source_target_pairs={{0,192},{32,224},{64,128},{96,160},{128,64},{160,96},{192,0},{224,... | collective-permute-start | bytes 98312 | tf_op jit(solution)/shard_map/ppermute | solution.py:26
  75.7 4.8 %collective-permute-start.4 = (f32[16,512]{1,0:T(8,128)S(1)}, f32[16,512]{1,0:T(8,128)S(1)}, u32[]{:S(2)}, u32[]{:S(2)}) collective-permute-start(f32[16,512]{1,0:T(8,128)S(1)} %add_multiply_fusion), channel_id=1, source_target_pairs={{0,32},{32,0},{64,96},{96,64},{128,160},{160,128},{192,224},{224,1... | collective-permute-start | bytes 98312 | tf_op jit(solution)/shard_map/ppermute | solution.py:26

commit v3 on v2

v3 whole, which is shorter than its diff:
```python
import functools
import math

import jax
import jax.numpy as jnp
from jax import lax
from jax.experimental import pallas as pl
from jax.experimental.pallas import tpu as pltpu
from jax.sharding import PartitionSpec as P

BF16, F32, I32 = jnp.bfloat16, jnp.float32, jnp.int32
ROUND_ROWS = 32
STEP_ROWS = 256
LOADS = 4

in_vmem = functools.partial(pl.BlockSpec, memory_space=pltpu.VMEM)
in_smem = functools.partial(pl.BlockSpec, memory_space=pltpu.SMEM)
in_place = functools.partial(pl.BlockSpec, memory_space=pl.ANY)


def params(mebibytes=12):
    return pltpu.CompilerParams(vmem_limit_bytes=mebibytes << 20)


def rows_of(a, b):
    return jnp.dot(a, b, preferred_element_type=F32)


def exchange(value, mask):
    return lax.ppermute(value, "row", [(i, i ^ mask) for i in range(lax.axis_size("row"))])


def pack_rows(features, panel_row, extra_rows, step):
    n_col = lax.axis_size("col")
    col_count, dim = features.shape
    count = panel_row.shape[1]
    n_extra = extra_rows[0].shape[0] if extra_rows else 0
    chunk = col_count // LOADS
    bits = col_count.bit_length() - 1
    assert col_count == 1 << bits

    def body(step_ref, panel_ref, *refs):
        extra, (features_hbm, out, rounds, table, tail, arrived) = refs[:-6], refs[-6:]
        loads = []
        for i in range(LOADS):
            part = pl.ds(i * chunk, chunk)
            loads.append(pltpu.make_async_copy(features_hbm.at[part], table.at[part], arrived.at[i]))
            loads[i].start()
        for core, source in enumerate(extra):
            @pl.when(lax.axis_index("row") % 2 == core)
            def _():
                pltpu.make_async_copy(source, tail, arrived.at[LOADS]).start()
        owner = lax.shift_right_logical(jnp.broadcast_to(panel_ref[...], (n_col, count)), bits)
        held = (owner == lax.broadcasted_iota(I32, (n_col, count), 0)).astype(I32)
        rounds[0] = (jnp.max(jnp.sum(held, axis=1, keepdims=True)) - 1) // ROUND_ROWS + 1
        place = jnp.broadcast_to(panel_ref[...], (8, count)) - lax.axis_index("col") * col_count
        owned = (place >= 0) & (place < col_count)
        lane = lax.broadcasted_iota(I32, (8, count), 1)
        running = owned.astype(I32)
        shift = 1
        while shift < count:
            running = running + jnp.where(lane >= shift, pltpu.roll(running, shift, axis=1), 0)
            shift *= 2
        slot = jnp.where(owned, running - 1 - step_ref[0] * ROUND_ROWS, -1)[:1]
        mine = slot == lax.broadcasted_iota(I32, (ROUND_ROWS, count), 0)
        wanted = jnp.sum(jnp.where(mine, place[:1] + 1, 0), axis=1, keepdims=True) - 1
        lane = lax.broadcasted_iota(I32, (ROUND_ROWS, chunk), 1)
        rows = jnp.zeros((ROUND_ROWS, dim), F32)
        for i in range(LOADS):
            pick = (wanted - i * chunk == lane).astype(F32).astype(BF16)
            loads[i].wait()
            rows = rows + rows_of(pick, table[pl.ds(i * chunk, chunk)])
        message = rows.astype(BF16)
        if extra:
            pltpu.make_async_copy(extra[0], tail, arrived.at[LOADS]).wait()
            message = jnp.concatenate([message, tail[...]], axis=0)
        for peer in range(n_col):
            out[peer] = message

    return pl.pallas_call(
        body,
        name="pack_rows",
        out_shape=(
            jax.ShapeDtypeStruct((n_col, ROUND_ROWS + n_extra, dim), BF16),
            jax.ShapeDtypeStruct((1,), I32),
        ),
        in_specs=[in_smem(), in_vmem()] + [in_place()] * len(extra_rows) + [in_place()],
        out_specs=(in_vmem(), in_smem()),
        scratch_shapes=[
            pltpu.VMEM((col_count, dim), BF16),
            pltpu.VMEM((max(n_extra, 16), dim), BF16),
            pltpu.SemaphoreType.DMA((LOADS + 1,)),
        ],
        compiler_params=params(),
    )(step, panel_row, *extra_rows, features)


def picks(panel_row, panel_column, bits, step, n_slots):
    count = panel_column.shape[0]
    owner_row = lax.shift_right_logical(panel_row, bits)
    owner = lax.shift_right_logical(panel_column, bits)
    before = lax.broadcasted_iota(I32, (count, count), 1) < lax.broadcasted_iota(I32, (count, count), 0)
    rank = jnp.sum(jnp.where(before & (owner == owner_row), 1, 0), axis=1, keepdims=True) - step * ROUND_ROWS
    slot = jnp.where((rank >= 0) & (rank < ROUND_ROWS), owner * ROUND_ROWS + rank, -1)
    return (slot == lax.broadcasted_iota(I32, (count, n_slots), 1)).astype(F32).astype(BF16)


def first_picks(panel_row, panel_column, col_count):
    n_slots = lax.axis_size("col") * ROUND_ROWS

    def body(row_ref, column_ref, out):
        out[...] = picks(row_ref[...], column_ref[...], col_count.bit_length() - 1, 0, n_slots)

    return pl.pallas_call(
        body,
        name="first_picks",
        out_shape=jax.ShapeDtypeStruct((panel_row.shape[1], n_slots), BF16),
        in_specs=[in_vmem(), in_vmem()],
        out_specs=in_vmem(),
        compiler_params=params(),
        cost_estimate=pl.CostEstimate(flops=8_000_000_000, transcendentals=0, bytes_accessed=32_000_000),
    )(panel_row, panel_column)


def panel_part(received):
    n_col, _, dim = received.shape
    return received[:, :ROUND_ROWS, :].reshape(n_col * ROUND_ROWS, dim)


def first_rows(pick, received, later):
    def body(pick_ref, received_ref, later_ref, out):
        rows = rows_of(pick_ref[...], panel_part(received_ref[...]))
        out[...] = (rows + later_ref[...].astype(F32)).astype(BF16)

    return pl.pallas_call(
        body,
        name="first_rows",
        out_shape=jax.ShapeDtypeStruct((pick.shape[0], received.shape[2]), BF16),
        in_specs=[in_vmem(), in_vmem(), in_vmem()],
        out_specs=in_vmem(),
        compiler_params=params(),
    )(pick, received, later)


def add_round(panel_row, panel_column, bits, received, panel, step):
    n_slots = received.shape[0] * ROUND_ROWS

    def body(step_ref, row_ref, column_ref, received_ref, panel_ref, out):
        pick = picks(row_ref[...], column_ref[...], bits, step_ref[0], n_slots)
        out[...] = (panel_ref[...].astype(F32) + rows_of(pick, panel_part(received_ref[...]))).astype(BF16)

    return pl.pallas_call(
        body,
        name="add_round",
        out_shape=jax.ShapeDtypeStruct(panel.shape, BF16),
        in_specs=[in_smem(), in_vmem(), in_vmem(), in_vmem(), in_vmem()],
        out_specs=in_vmem(),
        compiler_params=params(),
    )(step, panel_row, panel_column, received, panel)


def symmetric_matrix(received):
    dim = received.shape[2]

    def body(received_ref, out):
        raw = received_ref[:, ROUND_ROWS:, :].reshape(dim, dim).astype(F32)
        out[...] = ((raw + raw.T) * 0.5).astype(BF16)

    return pl.pallas_call(
        body,
        name="symmetric_matrix",
        out_shape=jax.ShapeDtypeStruct((dim, dim), BF16),
        in_specs=[in_vmem()],
        out_specs=in_vmem(),
        compiler_params=params(),
    )(received)


def pair_products(panel, kept_matrix, other_matrix, features, labels):
    count, dim = panel.shape
    col_count = features.shape[0]
    steps = count // STEP_ROWS

    def body(panel_ref, kept_ref, other_ref, features_ref, labels_hbm, kept, given, projected, sums, labels_ref, arrived):
        loads = []
        for i in range(steps):
            part = pl.ds(i * STEP_ROWS, STEP_ROWS)
            loads.append(pltpu.make_async_copy(labels_hbm.at[part], labels_ref.at[part], arrived.at[i]))
            loads[i].start()
        core = lax.axis_index("row") % 2
        rows = panel_ref[...]
        projected[core] = rows_of(rows, kept_ref[...]).astype(BF16)
        projected[1 - core] = rows_of(rows, other_ref[...]).astype(BF16)
        columns = features_ref[...]
        for i in range(steps):
            part = pl.ds(i * STEP_ROWS, STEP_ROWS)
            both = jnp.concatenate([projected[0, part], projected[1, part]], axis=0)
            pairs = lax.dot_general(both, columns, (((1,), (1,)), ((), ())), preferred_element_type=F32)
            loads[i].wait()
            probability = 1.0 / (1.0 + jnp.exp(-pairs[:STEP_ROWS]))
            residual = (probability - labels_ref[part].astype(F32)).astype(BF16)
            curvature = (probability * (1.0 - probability) * pairs[STEP_ROWS:]).astype(BF16)
            total = rows_of(jnp.concatenate([residual, curvature], axis=0), columns).astype(BF16)
            sums[0, part] = total[:STEP_ROWS]
            sums[1, part] = total[STEP_ROWS:]
        turned = rows.T
        for out, place in ((kept, core), (given, 1 - core)):
            half = rows_of(turned, sums[place])
            out[...] = (half + half.T).astype(out.dtype)

    return pl.pallas_call(
        body,
        name="pair_products",
        out_shape=(jax.ShapeDtypeStruct((dim, dim), F32), jax.ShapeDtypeStruct((dim, dim), BF16)),
        in_specs=[in_vmem()] * 4 + [in_place()],
        out_specs=(in_vmem(), in_vmem()),
        scratch_shapes=[
            pltpu.VMEM((2, count, dim), BF16),
            pltpu.VMEM((2, count, dim), BF16),
            pltpu.VMEM((count, col_count), I32),
            pltpu.SemaphoreType.DMA((steps,)),
        ],
        compiler_params=params(28),
    )(panel, kept_matrix, other_matrix, features, labels)


def shards(features, weight_raw, direction_raw, panel_index, labels):
    n_row, n_col = lax.axis_size("row"), lax.axis_size("col")
    col_count, dim = features.shape
    count = panel_index.shape[0]
    columns = features
    features, weight_raw, direction_raw, labels = (
        pltpu.with_memory_space_constraint(x, pltpu.HBM) for x in (features, weight_raw, direction_raw, labels)
    )
    panel_row = panel_index.reshape(1, count)
    first = jnp.zeros((1,), I32)
    sent, rounds = pack_rows(features, panel_row, (weight_raw, direction_raw), first)

    def another(state):
        step, rows = state
        fresh = lax.all_to_all(pack_rows(features, panel_row, (), step)[0], "col", 0, 0, tiled=True)
        column = panel_index.reshape(count, 1)
        return step + 1, add_round(panel_row, column, col_count.bit_length() - 1, fresh, rows, step)

    _, later = lax.while_loop(
        lambda state: state[0][0] < rounds[0], another, (first + 1, jnp.zeros((count, dim), BF16))
    )
    sent, later = lax.optimization_barrier((sent, later))
    received = lax.all_to_all(sent, "col", 0, 0, tiled=True)
    pick = first_picks(panel_row, panel_index.reshape(count, 1), col_count)
    received, pick = lax.optimization_barrier((received, pick))
    kept_matrix = symmetric_matrix(received)
    other_matrix = exchange(kept_matrix, 1)
    panel = first_rows(pick, received, later)
    kept, given = pair_products(panel, kept_matrix, other_matrix, columns, labels)
    chip_sum = (kept + exchange(given, 1).astype(F32)).astype(BF16)
    parts = lax.all_to_all(chip_sum.reshape(n_col, dim // n_col, dim), "col", 0, 0, tiled=True)
    mine = jnp.sum(parts.astype(F32), axis=0)
    near = mine + exchange(mine, 2)
    scale = 0.5 / math.sqrt(count * n_row * col_count * n_col)
    total = (near + exchange(near, 6)) * scale
    other = exchange(total, 1)
    on_first = lax.axis_index("row") % 2 == 0
    return jnp.where(on_first, total, other), jnp.where(on_first, other, total)


def solution(mesh):
    return jax.shard_map(
        shards,
        mesh=mesh,
        in_specs=(P("col", None), P("col", None), P("col", None), P("row"), P("row", "col")),
        out_specs=(P("col", None), P("col", None)),
        check_vma=False,
    )
```

time: 81.5 us -> 81.3 us (level)
  blocking collectives: 44.4 us -> 15.8 us
  waiting for transfers between devices: 5.72 us -> 26.4 us
  starting transfers between devices: 13.9 us -> 23.5 us
  local copies, waits for them, and re-layouts: 1.62 us -> 0.19 us
    all_to_all x1 -> x0, blocking collectives: 30.2 us -> none  [shards(): received = lax.all_to_all(sent, 'col', 0, 0, tiled=True)]
    all_to_all x0 -> x1, waiting for transfers between devices: none -> 20.2 us  [shards(): received = lax.all_to_all(sent, 'col', 0, 0, tiled=True)]
    all_to_all x0 -> x1, starting transfers between devices: none -> 9.24 us  [shards(): received = lax.all_to_all(sent, 'col', 0, 0, tiled=True)]
    all_to_all x1, blocking collectives: 14.3 us -> 15.8 us  [shards(): lax.all_to_all(chip_sum.reshape(n_col, dim // n_col, dim), 'col', 0, 0, t...]
    unnamed x8 -> x4, local copies, waits for them, and re-layouts: 1.44 us -> 0.01 us
  transfers between devices with their start and end apart: 5 -> 6, of which waited for: 4 -> 6; matrix products, arithmetic and copies ran while one was open for 0% -> 0% of each run, Pallas kernels for 2% -> 1%
where the time goes in v3:
time: 81.3 us; the launch traced here: 81 us
  waiting for transfers between devices  26.4 us (32%)
  starting transfers between devices  23.5 us (29%)
  blocking collectives  15.8 us (19%)
  Pallas kernels  12.9 us (16%)
  other arithmetic  0.89 us (1%)
    all_to_all x1, waiting for transfers between devices, shards(): received = lax.all_to_all(sent, 'col', 0, 0, tiled=True)  20.2 us
    all_to_all x1, blocking collectives, shards(): lax.all_to_all(chip_sum.reshape(n_col, dim // n_col, dim), 'col', 0, 0, t...  15.8 us
    ppermute x5, starting transfers between devices, exchange(): lax.ppermute(value, 'row', [(i, i ^ mask) for i in range(lax.axis_size('r...  14.3 us
    all_to_all x1, starting transfers between devices, shards(): received = lax.all_to_all(sent, 'col', 0, 0, tiled=True)  9.24 us
    pallas_call x1, Pallas kernels, pair_products(): pl.pallas_call(body, name='pair_products', out_shape=(jax.ShapeDtypeStruc...  7.48 us
    ppermute x5, waiting for transfers between devices, exchange(): lax.ppermute(value, 'row', [(i, i ^ mask) for i in range(lax.axis_size('r...  6.19 us
    pallas_call x1, Pallas kernels, pack_rows(): pl.pallas_call(body, name='pack_rows', out_shape=(jax.ShapeDtypeStruct((n...  4 us
  transfers between devices with their start and end apart: 6, of which 6 were waited for; matrix products, arithmetic and copies ran while one was open for 0% of the time, Pallas kernels for 1%

profile of v3, /device:TPU:1, one launch (start us, length us, event | category | flops | bytes accessed | tf_op | source)
XLA Modules:
  0.0 81.0 jit_solution(16899089191821261435)
XLA Ops:
  0.6 0.0 copy-start.1
  0.6 4.0 %pack_rows.2 = (bf16[32,48,512]{2,1,0:T(8,128)(2,1)}, s32[1]{0:T(128)}) custom-call(s32[1]{0:T(128)} %constant.27.clone.1.step_ref, s32[1,512]{1,0:T(1,128)} %bitcast.8, bf16[16,512]{1,0:T(8,128)(2,1)} %refs_0_.1, bf16[16,512]{1,0:T(8,128)(2,1)} %refs_1_.1, bf16[2048,512]{1,0:T(8,128)(2,1)} %features_ref.1), custom_call_target="tpu_custom_call" | custom-call | tf_op jit(solution)/shard_map/pack_rows/pallas_call | solution.py:80
  4.7 0.0 copy-done.1
  4.7 0.7 while.10
  5.4 9.2 %all-to-all-start.1 = ((bf16[32,48,512]{2,1,0:T(8,128)(2,1)}), bf16[32,48,512]{2,1,0:T(8,128)(2,1)S(1)}, u32[]{:S(2)}, u32[]{:S(2)}) async-start(bf16[32,48,512]{2,1,0:T(8,128)(2,1)} %get-tuple-element.47), calls=%async_computation.1 | async-start | bytes 3145728 | tf_op jit(solution)/shard_map/all_to_all | solution.py:249
  14.6 0.1 copy.8.column_ref
  14.8 0.5 first_picks.1.pick_ref
  15.3 20.2 %all-to-all-done.1.received_ref = bf16[32,48,512]{2,1,0:T(8,128)(2,1)S(1)} async-done(((bf16[32,48,512]{2,1,0:T(8,128)(2,1)}), bf16[32,48,512]{2,1,0:T(8,128)(2,1)S(1)}, u32[]{:S(2)}, u32[]{:S(2)}) %all-to-all-start.1) | async-done | bytes 1572896 | tf_op jit(solution)/shard_map/all_to_all | solution.py:249
  35.5 0.2 symmetric_matrix.1.kept_ref
  35.7 0.0 copy-start
  35.7 2.3 %collective-permute-start = (bf16[512,512]{1,0:T(8,128)(2,1)S(1)}, bf16[512,512]{1,0:T(8,128)(2,1)S(1)}, u32[]{:S(2)}, u32[]{:S(2)}) collective-permute-start(bf16[512,512]{1,0:T(8,128)(2,1)S(1)} %symmetric_matrix.1.kept_ref), channel_id=1, source_target_pairs={{0,32},{32,0},{64,96},{96,64},{128,160},{160,128},{192,224},{224,1... | collective-permute-start | bytes 1572872 | tf_op jit(solution)/shard_map/ppermute | solution.py:30
  38.0 0.7 first_rows.1.panel_ref
  38.7 0.8 %collective-permute-done.other_ref = bf16[512,512]{1,0:T(8,128)(2,1)S(1)} collective-permute-done((bf16[512,512]{1,0:T(8,128)(2,1)S(1)}, bf16[512,512]{1,0:T(8,128)(2,1)S(1)}, u32[]{:S(2)}, u32[]{:S(2)}) %collective-permute-start) | collective-permute-done | bytes 524320 | tf_op jit(solution)/shard_map/ppermute | solution.py:30
  39.6 0.0 copy-done
  39.6 7.5 %pair_products.1 = (f32[512,512]{1,0:T(8,128)S(1)}, bf16[512,512]{1,0:T(8,128)(2,1)S(1)}) custom-call(bf16[512,512]{1,0:T(8,128)(2,1)S(1)} %first_rows.1.panel_ref, bf16[512,512]{1,0:T(8,128)(2,1)S(1)} %symmetric_matrix.1.kept_ref, bf16[512,512]{1,0:T(8,128)(2,1)S(1)} %collective-permute-done.other_ref, bf16[2048,512]{1,0:T(8,128)(2,1)S(1)} %copy-done, ...), custom_call_target="tpu_custom_call" | custom-call | tf_op jit(solution)/shard_map/pair_products/pallas_call | solution.py:211
  47.0 0.5 collective-permute-start.1
  47.5 1.5 %collective-permute-done.1 = bf16[512,512]{1,0:T(8,128)(2,1)S(1)} collective-permute-done((bf16[512,512]{1,0:T(8,128)(2,1)S(1)}, bf16[512,512]{1,0:T(8,128)(2,1)S(1)}, u32[]{:S(2)}, u32[]{:S(2)}) %collective-permute-start.1) | collective-permute-done | bytes 524320 | tf_op jit(solution)/shard_map/ppermute | solution.py:30
  49.0 0.2 add_convert_fusion
  49.2 15.8 %all_to_all.15 = bf16[32,16,512]{2,1,0:T(8,128)(2,1)S(1)} all-to-all(bf16[32,16,512]{2,1,0:T(8,128)(2,1)S(1)} %bitcast.7), channel_id=1, replica_groups=mesh['row'=8,'col'=32] {'col'}, dimensions={0} | all-to-all | bytes 1048576 | tf_op jit(solution)/shard_map/all_to_all | solution.py:257
  65.0 0.1 convert_reduce_fusion
  65.0 3.1 %collective-permute-start.2 = (f32[16,512]{1,0:T(8,128)S(1)}, f32[16,512]{1,0:T(8,128)S(1)}, u32[]{:S(2)}, u32[]{:S(2)}) collective-permute-start(f32[16,512]{1,0:T(8,128)S(1)} %convert_reduce_fusion), channel_id=1, source_target_pairs={{0,64},{32,96},{64,0},{96,32},{128,192},{160,224},{192,128},{224,1... | collective-permute-start | bytes 98312 | tf_op jit(solution)/shard_map/ppermute | solution.py:30
  68.1 1.7 %collective-permute-done.2 = f32[16,512]{1,0:T(8,128)S(1)} collective-permute-done((f32[16,512]{1,0:T(8,128)S(1)}, f32[16,512]{1,0:T(8,128)S(1)}, u32[]{:S(2)}, u32[]{:S(2)}) %collective-permute-start.2) | collective-permute-done | bytes 32800 | tf_op jit(solution)/shard_map/ppermute | solution.py:30
  69.8 4.1 %collective-permute-start.3 = (f32[16,512]{1,0:T(8,128)S(1)}, f32[16,512]{1,0:T(8,128)S(1)}, u32[]{:S(2)}, u32[]{:S(2)}) collective-permute-start(f32[16,512]{1,0:T(8,128)S(1)} %add.18), channel_id=1, source_target_pairs={{0,192},{32,224},{64,128},{96,160},{128,64},{160,96},{192,0},{224,... | collective-permute-start | bytes 98312 | tf_op jit(solution)/shard_map/ppermute | solution.py:30
  73.9 1.3 %collective-permute-done.3 = f32[16,512]{1,0:T(8,128)S(1)} collective-permute-done((f32[16,512]{1,0:T(8,128)S(1)}, f32[16,512]{1,0:T(8,128)S(1)}, u32[]{:S(2)}, u32[]{:S(2)}) %collective-permute-start.3) | collective-permute-done | bytes 32800 | tf_op jit(solution)/shard_map/ppermute | solution.py:30
  75.2 4.3 %collective-permute-start.4 = (f32[16,512]{1,0:T(8,128)S(1)}, f32[16,512]{1,0:T(8,128)S(1)}, u32[]{:S(2)}, u32[]{:S(2)}) collective-permute-start(f32[16,512]{1,0:T(8,128)S(1)} %add_multiply_fusion), channel_id=1, source_target_pairs={{0,32},{32,0},{64,96},{96,64},{128,160},{160,128},{192,224},{224,1... | collective-permute-start | bytes 98312 | tf_op jit(solution)/shard_map/ppermute | solution.py:30
  79.5 0.9 %collective-permute-done.4 = f32[16,512]{1,0:T(8,128)S(1)} collective-permute-done((f32[16,512]{1,0:T(8,128)S(1)}, f32[16,512]{1,0:T(8,128)S(1)}, u32[]{:S(2)}, u32[]{:S(2)}) %collective-permute-start.4) | collective-permute-done | bytes 32800 | tf_op jit(solution)/shard_map/ppermute | solution.py:30
  80.4 0.6 broadcast_select_fusion
  (3 shorter events, 0.1 us)
Async XLA Ops:
  0.6 4.1 %copy-start.1 = (s32[512]{0:T(512)S(1)}, s32[512]{0:T(512)}, u32[]{:S(2)}) copy-start(s32[512]{0:T(512)} %param.10) | copy-start | bytes 6148
  5.4 30.1 %all-to-all-start.1 = ((bf16[32,48,512]{2,1,0:T(8,128)(2,1)}), bf16[32,48,512]{2,1,0:T(8,128)(2,1)S(1)}, u32[]{:S(2)}, u32[]{:S(2)}) async-start(bf16[32,48,512]{2,1,0:T(8,128)(2,1)} %get-tuple-element.47), calls=%async_computation.1 | async-start | bytes 3145728 | tf_op jit(solution)/shard_map/all_to_all | solution.py:249
  35.7 3.8 %copy-start = (bf16[2048,512]{1,0:T(8,128)(2,1)S(1)}, bf16[2048,512]{1,0:T(8,128)(2,1)}, u32[]{:S(2)}) copy-start(bf16[2048,512]{1,0:T(8,128)(2,1)} %get-tuple-element.126) | copy-start | bytes 6291460
  35.7 3.8 %collective-permute-start = (bf16[512,512]{1,0:T(8,128)(2,1)S(1)}, bf16[512,512]{1,0:T(8,128)(2,1)S(1)}, u32[]{:S(2)}, u32[]{:S(2)}) collective-permute-start(bf16[512,512]{1,0:T(8,128)(2,1)S(1)} %symmetric_matrix.1.kept_ref), channel_id=1, source_target_pairs={{0,32},{32,0},{64,96},{96,64},{128,160},{160,128},{192,224},{224,1... | collective-permute-start | bytes 1572872 | tf_op jit(solution)/shard_map/ppermute | solution.py:30
  47.0 2.0 %collective-permute-start.1 = (bf16[512,512]{1,0:T(8,128)(2,1)S(1)}, bf16[512,512]{1,0:T(8,128)(2,1)S(1)}, u32[]{:S(2)}, u32[]{:S(2)}) collective-permute-start(bf16[512,512]{1,0:T(8,128)(2,1)S(1)} %get-tuple-element.52), channel_id=1, source_target_pairs={{0,32},{32,0},{64,96},{96,64},{128,160},{160,128},{192,224},{224,1... | collective-permute-start | bytes 1572872 | tf_op jit(solution)/shard_map/ppermute | solution.py:30
  65.0 4.7 %collective-permute-start.2 = (f32[16,512]{1,0:T(8,128)S(1)}, f32[16,512]{1,0:T(8,128)S(1)}, u32[]{:S(2)}, u32[]{:S(2)}) collective-permute-start(f32[16,512]{1,0:T(8,128)S(1)} %convert_reduce_fusion), channel_id=1, source_target_pairs={{0,64},{32,96},{64,0},{96,32},{128,192},{160,224},{192,128},{224,1... | collective-permute-start | bytes 98312 | tf_op jit(solution)/shard_map/ppermute | solution.py:30
  69.8 5.4 %collective-permute-start.3 = (f32[16,512]{1,0:T(8,128)S(1)}, f32[16,512]{1,0:T(8,128)S(1)}, u32[]{:S(2)}, u32[]{:S(2)}) collective-permute-start(f32[16,512]{1,0:T(8,128)S(1)} %add.18), channel_id=1, source_target_pairs={{0,192},{32,224},{64,128},{96,160},{128,64},{160,96},{192,0},{224,... | collective-permute-start | bytes 98312 | tf_op jit(solution)/shard_map/ppermute | solution.py:30
  75.2 5.2 %collective-permute-start.4 = (f32[16,512]{1,0:T(8,128)S(1)}, f32[16,512]{1,0:T(8,128)S(1)}, u32[]{:S(2)}, u32[]{:S(2)}) collective-permute-start(f32[16,512]{1,0:T(8,128)S(1)} %add_multiply_fusion), channel_id=1, source_target_pairs={{0,32},{32,0},{64,96},{96,64},{128,160},{160,128},{192,224},{224,1... | collective-permute-start | bytes 98312 | tf_op jit(solution)/shard_map/ppermute | solution.py:30
